TPU v7x, 32 devices: a whole 2x2x4 slice. The times are simulated.
32 devices in a mesh: section: 4 (over x, core), row: 4 (over z), col: 2 (over y).
Axes of the slice: x: 2, y: 2, z: 4, core: 2. Of those that a mesh axis runs over, the one named last changes fastest.
Arguments:
- latents: bfloat16 [2, 1280, 4, 128], P(None, 'col', 'row'), may hold values from -6 to 6
- timesteps: int32 [2], replicated, may hold values from 0 to 999
- weights: bfloat16 [4, 1280, 1280], P('section', 'row', 'col'), may hold values from -0.15625 to 0.15625
- taps: float32 [4, 3, 1280], P('section'), may hold values from -3 to 3
- time_table: bfloat16 [4, 1000, 1280], P('section'), may hold values from -5 to 5
- dilations: int32 [4], P('section'), may hold values from 1 to 4
Outputs:
- acts: bfloat16 [4, 2, 1280, 4, 128], P('section', None, 'col', 'row')
All inputs are finite; a program needn't handle non-finite values.
Results may differ from a plain program's by a relative error of at most 0.03.
Values may be sent and summed in bfloat16 or wider, within the bound.
A program may use at most 64 MiB of HBM per device.

v0:
```python
import jax
import jax.numpy as jnp
from jax import lax
from jax.sharding import PartitionSpec as P

DMAX = 4


def shifted(value, axis, steps):
    count = lax.axis_size(axis)
    first, last = (max(0, -steps), min(count, count - steps))
    return lax.ppermute(value, axis, [(source, source + steps) for source in range(first, last)])


def from_partner(block, axis, distance):
    count = lax.axis_size(axis)
    route = []
    for low in range(count):
        high = low | 1 << distance
        if high != low and high < count:
            route += [(low, high), (high, low)]
    return lax.ppermute(block, axis, route)


def activate(current, tap_rows, embedding, dilation, frame_count):
    widened = current.astype(jnp.float32)
    padded = jnp.pad(widened, ((0, 0), (0, 0), (DMAX, DMAX)))
    earlier = lax.dynamic_slice_in_dim(padded, DMAX - dilation, frame_count, 2)
    later_frames = lax.dynamic_slice_in_dim(padded, DMAX + dilation, frame_count, 2)
    summed = (
        tap_rows[0][:, None, None] * earlier
        + tap_rows[1][:, None, None] * widened
        + tap_rows[2][:, None, None] * later_frames
        + embedding[:, None, None]
    )
    return jax.nn.silu(summed).astype(jnp.bfloat16)


def per_device(latents, timesteps, weights, taps, time_table, dilations):
    section_count = lax.axis_size("section")
    section_id = lax.axis_index("section")
    col_index = lax.axis_index("col")
    micro_count = latents.shape[0]
    local_channels = latents.shape[1]
    frame_count = latents.shape[3]
    midpoint = section_count // 2
    bit_total = section_count.bit_length() - 1
    matrix_cols = lax.all_gather(weights[0], "row", axis=0, tiled=True)
    tap_all = taps[0]
    time_rows = time_table[0]
    dilation = dilations[0]

    def advance(tick_id, state_tuple, with_skip):
        incoming, kept, skip_store = state_tuple
        micro_id = tick_id - section_id
        active = (micro_id >= 0) & (micro_id < micro_count)
        slot_id = jnp.clip(micro_id, 0, micro_count - 1)
        entering = lax.dynamic_index_in_dim(latents, slot_id, 0, keepdims=False)
        current = jnp.where(section_id == 0, entering, incoming)
        step_id = lax.dynamic_index_in_dim(timesteps, slot_id, 0, keepdims=False)
        embedding = lax.dynamic_index_in_dim(time_rows, step_id, 0, keepdims=False).astype(
            jnp.float32
        )
        tap_mine = lax.dynamic_slice_in_dim(tap_all, col_index * local_channels, local_channels, 1)
        embed_mine = lax.dynamic_slice_in_dim(
            embedding, col_index * local_channels, local_channels, 0
        )
        activated = lax.all_gather(
            activate(current, tap_mine, embed_mine, dilation, frame_count),
            "col",
            axis=0,
            tiled=True,
        )
        mixed = lax.dot_general(
            matrix_cols,
            activated.reshape(activated.shape[0], -1),
            (((0,), (0,)), ((), ())),
            preferred_element_type=jnp.float32,
        ).reshape(current.shape)
        stored_skip = lax.dynamic_index_in_dim(skip_store, slot_id, 0, keepdims=False).astype(
            jnp.float32
        )
        skip_term = jnp.where(section_id >= midpoint, stored_skip, 0.0)
        result = (current.astype(jnp.float32) + mixed + skip_term).astype(jnp.bfloat16)
        previous = lax.dynamic_index_in_dim(kept, slot_id, 0, keepdims=False)
        kept = lax.dynamic_update_index_in_dim(
            kept, jnp.where(active, result, previous), slot_id, 0
        )
        incoming = shifted(result, "section", 1)
        if with_skip:
            mirrored = result
            bit_order = list(range(bit_total))
            for bit_number in bit_order:
                mirrored = from_partner(mirrored, "section", bit_number)
            source_micro = tick_id - (section_count - 1 - section_id)
            usable = (section_id >= midpoint) & (source_micro >= 0) & (source_micro < micro_count)
            source_slot = jnp.clip(source_micro, 0, micro_count - 1)
            held = lax.dynamic_index_in_dim(skip_store, source_slot, 0, keepdims=False)
            skip_store = lax.dynamic_update_index_in_dim(
                skip_store, jnp.where(usable, mirrored, held), source_slot, 0
            )
        return (incoming, kept, skip_store)

    blank = jnp.zeros(latents.shape[1:], jnp.bfloat16)
    initial = (
        blank,
        jnp.zeros(latents.shape, jnp.bfloat16),
        jnp.zeros(latents.shape, jnp.bfloat16),
    )
    first_end = micro_count + midpoint - 1
    state_tuple = lax.fori_loop(
        0, first_end, lambda tick_id, carried: advance(tick_id, carried, True), initial
    )
    state_tuple = lax.fori_loop(
        first_end,
        micro_count + section_count - 1,
        lambda tick_id, carried: advance(tick_id, carried, False),
        state_tuple,
    )
    return state_tuple[1][None]


def solution(mesh):
    in_specs = (
        P(None, "col", "row", None),
        P(),
        P("section", "row", "col"),
        P("section", None, None),
        P("section", None, None),
        P("section"),
    )
    out_specs = P("section", None, "col", "row", None)
    return jax.shard_map(
        per_device, mesh=mesh, in_specs=in_specs, out_specs=out_specs, check_vma=False
    )
```

profile of v0, /device:TPU:1, one launch (start us, length us, event | category | flops | bytes accessed | tf_op | source)
XLA Modules:
  0.0 153.2 jit_solution(2454798220183565018)
XLA Ops:
  6.5 0.0 copy-start
  6.5 0.0 all-gather.3.cloned.1.call-start
  6.5 0.7 all-gather.3.cloned.1.call-update
  7.9 0.0 copy-done
  8.0 1.2 copy.7
  9.2 40.0 %all-gather.3.cloned.1.call-done = bf16[1,1280,640]{2,1,0:T(8,128)(2,1)} async-done(((bf16[1,320,640]{2,1,0:T(8,128)(2,1)}), bf16[1,1280,640]{2,1,0:T(8,128)(2,1)}) %all-gather.3.cloned.1.call-update) | async-done | bytes 1638416 | tf_op jit(solution)/shard_map/all_gather | solution.py:48
  49.2 0.0 copy-done.3
  49.2 61.1 %while.38 = (s32[]{:T(128)}, bf16[640,1,128]{0,2,1:T(8,128)(2,1)S(1)}, bf16[2,640,1,128]{1,3,2,0:T(8,128)(2,1)S(1)}, bf16[2,640,1,128]{1,3,2,0:T(8,128)(2,1)S(1)...) while((s32[]{:T(128)}, ...), condition=%wide.region_1.2_spmd, body=%wide.region_0.1_spmd.sunk | while | flops 211354256 | bytes 14284052 | solution.py:111
  49.3 0.0 copy-start.1
  49.3 0.6 dynamic_slice.274
  51.9 0.8 slice_reduce_fusion.8
  52.7 0.2 multiply_convert_fusion.4
  52.9 5.7 %all_gather.28 = bf16[1280,1,128]{0,2,1:T(8,128)(2,1)S(1)} all-gather(bf16[640,1,128]{0,2,1:T(8,128)(2,1)S(1)} %multiply_convert_fusion.4), channel_id=1, replica_groups=mesh['section'=4,'row'=4,'col'=2] {'col'}, dimensions={0}, use_global_device_ids=true | all-gather | bytes 491520 | tf_op jit(solution)/shard_map/while/body/eval_jaxpr/all_gather | solution.py:68
  58.6 0.0 copy-done.1
  58.6 1.1 bitcast_dynamic-update-slice_fusion.6
  59.7 1.6 %collective-permute-start.1 = (bf16[640,1,128]{0,2,1:T(8,128)(2,1)}, bf16[640,1,128]{0,2,1:T(8,128)(2,1)S(1)}, u32[]{:S(2)}, u32[]{:S(2)}) collective-permute-start(bf16[640,1,128]{0,2,1:T(8,128)(2,1)} %get-tuple-element.1072), channel_id=1, source_target_pairs={{0,8},{8,0},{16,24},{24,16},{1,9},{9,1},{17,25},{25,17},{2,10},{10... | collective-permute-start | bytes 491528 | tf_op jit(solution)/shard_map/while/body/eval_jaxpr/ppermute | solution.py:22
  61.3 1.2 collective-permute-done.1
  62.5 1.2 collective-permute-start.2
  63.7 2.7 %collective-permute-start = (bf16[640,1,128]{0,2,1:T(8,128)(2,1)}, bf16[640,1,128]{0,2,1:T(8,128)(2,1)S(1)}, u32[]{:S(2)}, u32[]{:S(2)}) collective-permute-start(bf16[640,1,128]{0,2,1:T(8,128)(2,1)} %get-tuple-element.1072), channel_id=1, source_target_pairs={{0,8},{8,16},{16,24},{1,9},{9,17},{17,25},{2,10},{10,18},{18,26},{... | collective-permute-start | bytes 491528 | tf_op jit(solution)/shard_map/while/body/eval_jaxpr/ppermute | solution.py:12
  66.5 1.5 collective-permute-done.2
  68.0 0.1 bitcast_dynamic-update-slice_fusion.7
  68.0 1.6 %collective-permute-done = bf16[640,1,128]{0,2,1:T(8,128)(2,1)S(1)} collective-permute-done((bf16[640,1,128]{0,2,1:T(8,128)(2,1)}, bf16[640,1,128]{0,2,1:T(8,128)(2,1)S(1)}, u32[]{:S(2)}, u32[]{:S(2)}) %collective-permute-start) | collective-permute-done | bytes 163872 | tf_op jit(solution)/shard_map/while/body/eval_jaxpr/ppermute | solution.py:12
  69.6 0.6 dynamic_slice.274
  72.2 0.8 slice_reduce_fusion.8
  73.0 0.2 multiply_convert_fusion.4
  73.2 6.8 %all_gather.28 = bf16[1280,1,128]{0,2,1:T(8,128)(2,1)S(1)} all-gather(bf16[640,1,128]{0,2,1:T(8,128)(2,1)S(1)} %multiply_convert_fusion.4), channel_id=1, replica_groups=mesh['section'=4,'row'=4,'col'=2] {'col'}, dimensions={0}, use_global_device_ids=true | all-gather | bytes 491520 | tf_op jit(solution)/shard_map/while/body/eval_jaxpr/all_gather | solution.py:68
  80.0 0.0 copy-done.1
  80.0 1.1 bitcast_dynamic-update-slice_fusion.6
  81.1 0.5 collective-permute-start.1
  81.6 1.2 collective-permute-done.1
  82.9 1.2 collective-permute-start.2
  84.1 2.7 %collective-permute-start = (bf16[640,1,128]{0,2,1:T(8,128)(2,1)}, bf16[640,1,128]{0,2,1:T(8,128)(2,1)S(1)}, u32[]{:S(2)}, u32[]{:S(2)}) collective-permute-start(bf16[640,1,128]{0,2,1:T(8,128)(2,1)} %get-tuple-element.1072), channel_id=1, source_target_pairs={{0,8},{8,16},{16,24},{1,9},{9,17},{17,25},{2,10},{10,18},{18,26},{... | collective-permute-start | bytes 491528 | tf_op jit(solution)/shard_map/while/body/eval_jaxpr/ppermute | solution.py:12
  86.8 1.5 collective-permute-done.2
  88.3 0.1 bitcast_dynamic-update-slice_fusion.7
  88.4 1.6 %collective-permute-done = bf16[640,1,128]{0,2,1:T(8,128)(2,1)S(1)} collective-permute-done((bf16[640,1,128]{0,2,1:T(8,128)(2,1)}, bf16[640,1,128]{0,2,1:T(8,128)(2,1)S(1)}, u32[]{:S(2)}, u32[]{:S(2)}) %collective-permute-start) | collective-permute-done | bytes 163872 | tf_op jit(solution)/shard_map/while/body/eval_jaxpr/ppermute | solution.py:12
  90.0 0.6 dynamic_slice.274
  92.5 0.8 slice_reduce_fusion.8
  93.4 0.2 multiply_convert_fusion.4
  93.6 6.8 %all_gather.28 = bf16[1280,1,128]{0,2,1:T(8,128)(2,1)S(1)} all-gather(bf16[640,1,128]{0,2,1:T(8,128)(2,1)S(1)} %multiply_convert_fusion.4), channel_id=1, replica_groups=mesh['section'=4,'row'=4,'col'=2] {'col'}, dimensions={0}, use_global_device_ids=true | all-gather | bytes 491520 | tf_op jit(solution)/shard_map/while/body/eval_jaxpr/all_gather | solution.py:68
  100.4 1.1 bitcast_dynamic-update-slice_fusion.6
  101.5 0.5 collective-permute-start.1
  102.0 1.2 collective-permute-done.1
  103.2 1.2 collective-permute-start.2
  104.4 2.7 %collective-permute-start = (bf16[640,1,128]{0,2,1:T(8,128)(2,1)}, bf16[640,1,128]{0,2,1:T(8,128)(2,1)S(1)}, u32[]{:S(2)}, u32[]{:S(2)}) collective-permute-start(bf16[640,1,128]{0,2,1:T(8,128)(2,1)} %get-tuple-element.1072), channel_id=1, source_target_pairs={{0,8},{8,16},{16,24},{1,9},{9,17},{17,25},{2,10},{10,18},{18,26},{... | collective-permute-start | bytes 491528 | tf_op jit(solution)/shard_map/while/body/eval_jaxpr/ppermute | solution.py:12
  107.2 1.5 collective-permute-done.2
  108.7 0.1 bitcast_dynamic-update-slice_fusion.7
  108.7 1.6 %collective-permute-done = bf16[640,1,128]{0,2,1:T(8,128)(2,1)S(1)} collective-permute-done((bf16[640,1,128]{0,2,1:T(8,128)(2,1)}, bf16[640,1,128]{0,2,1:T(8,128)(2,1)S(1)}, u32[]{:S(2)}, u32[]{:S(2)}) %collective-permute-start) | collective-permute-done | bytes 163872 | tf_op jit(solution)/shard_map/while/body/eval_jaxpr/ppermute | solution.py:12
  110.3 35.1 %while.39 = (s32[]{:T(128)}, bf16[640,1,128]{0,2,1:T(8,128)(2,1)S(1)}, bf16[2,640,1,128]{1,3,2,0:T(8,128)(2,1)S(1)}, pred[]{:T(512)}, s32[]{:T(128)}, /*index=5*...) while((s32[]{:T(128)}, ...), condition=%wide.region_3.4_spmd, body=%wide.region_2.3_spmd.sunk | while | flops 211272336 | bytes 12153995 | solution.py:114
  110.3 0.6 dynamic_slice.279
  112.9 0.8 slice_reduce_fusion.9
  113.7 0.2 multiply_convert_fusion.5
  113.9 6.8 %all_gather.29 = bf16[1280,1,128]{0,2,1:T(8,128)(2,1)S(1)} all-gather(bf16[640,1,128]{0,2,1:T(8,128)(2,1)S(1)} %multiply_convert_fusion.5), channel_id=1, replica_groups=mesh['section'=4,'row'=4,'col'=2] {'col'}, dimensions={0}, use_global_device_ids=true | all-gather | bytes 491520 | tf_op jit(solution)/shard_map/while/body/eval_jaxpr/all_gather | solution.py:68
  120.7 1.1 bitcast_dynamic-update-slice_fusion.8
  121.8 3.5 %collective-permute-start.3 = (bf16[640,1,128]{0,2,1:T(8,128)(2,1)}, bf16[640,1,128]{0,2,1:T(8,128)(2,1)S(1)}, u32[]{:S(2)}, u32[]{:S(2)}) collective-permute-start(bf16[640,1,128]{0,2,1:T(8,128)(2,1)} %get-tuple-element.1093), channel_id=1, source_target_pairs={{0,8},{8,16},{16,24},{1,9},{9,17},{17,25},{2,10},{10,18},{18,26},{... | collective-permute-start | bytes 491528 | tf_op jit(solution)/shard_map/while/body/eval_jaxpr/ppermute | solution.py:12
  125.3 2.6 %collective-permute-done.3 = bf16[640,1,128]{0,2,1:T(8,128)(2,1)S(1)} collective-permute-done((bf16[640,1,128]{0,2,1:T(8,128)(2,1)}, bf16[640,1,128]{0,2,1:T(8,128)(2,1)S(1)}, u32[]{:S(2)}, u32[]{:S(2)}) %collective-permute-start.3) | collective-permute-done | bytes 163872 | tf_op jit(solution)/shard_map/while/body/eval_jaxpr/ppermute | solution.py:12
  127.9 0.6 dynamic_slice.279
  130.5 0.8 slice_reduce_fusion.9
  131.3 0.2 multiply_convert_fusion.5
  131.5 4.8 %all_gather.29 = bf16[1280,1,128]{0,2,1:T(8,128)(2,1)S(1)} all-gather(bf16[640,1,128]{0,2,1:T(8,128)(2,1)S(1)} %multiply_convert_fusion.5), channel_id=1, replica_groups=mesh['section'=4,'row'=4,'col'=2] {'col'}, dimensions={0}, use_global_device_ids=true | all-gather | bytes 491520 | tf_op jit(solution)/shard_map/while/body/eval_jaxpr/all_gather | solution.py:68
  136.3 0.0 copy-done.2
  136.4 1.1 bitcast_dynamic-update-slice_fusion.8
  137.5 5.4 %collective-permute-start.3 = (bf16[640,1,128]{0,2,1:T(8,128)(2,1)}, bf16[640,1,128]{0,2,1:T(8,128)(2,1)S(1)}, u32[]{:S(2)}, u32[]{:S(2)}) collective-permute-start(bf16[640,1,128]{0,2,1:T(8,128)(2,1)} %get-tuple-element.1093), channel_id=1, source_target_pairs={{0,8},{8,16},{16,24},{1,9},{9,17},{17,25},{2,10},{10,18},{18,26},{... | collective-permute-start | bytes 491528 | tf_op jit(solution)/shard_map/while/body/eval_jaxpr/ppermute | solution.py:12
  142.9 2.6 %collective-permute-done.3 = bf16[640,1,128]{0,2,1:T(8,128)(2,1)S(1)} collective-permute-done((bf16[640,1,128]{0,2,1:T(8,128)(2,1)}, bf16[640,1,128]{0,2,1:T(8,128)(2,1)S(1)}, u32[]{:S(2)}, u32[]{:S(2)}) %collective-permute-start.3) | collective-permute-done | bytes 163872 | tf_op jit(solution)/shard_map/while/body/eval_jaxpr/ppermute | solution.py:12
  145.5 0.9 copy.9
  (25 shorter events, 0.4 us)
Async XLA Ops:
  6.5 1.4 copy-start
  6.5 42.7 %copy-start.3 = (s32[2]{0:T(128)S(1)}, s32[2]{0:T(128)}, u32[]{:S(2)}) copy-start(s32[2]{0:T(128)} %param.11) | copy-start | bytes 28
  6.5 42.6 %all-gather.3.cloned.1.call-start = ((), (), s32[]{:S(2)}) async-start(), calls=%async_computation | async-start | bytes 2048000 | tf_op jit(solution)/shard_map/all_gather | solution.py:48
  49.3 9.3 %copy-start.1 = (bf16[1280,640]{1,0:T(8,128)(2,1)S(1)}, bf16[1280,640]{1,0:T(8,128)(2,1)}, u32[]{:S(2)}) copy-start(bf16[1280,640]{1,0:T(8,128)(2,1)} %get-tuple-element.1148) | copy-start | bytes 4915204 | tf_op jit(solution)/shard_map/while
  59.7 2.9 %collective-permute-start.1 = (bf16[640,1,128]{0,2,1:T(8,128)(2,1)}, bf16[640,1,128]{0,2,1:T(8,128)(2,1)S(1)}, u32[]{:S(2)}, u32[]{:S(2)}) collective-permute-start(bf16[640,1,128]{0,2,1:T(8,128)(2,1)} %get-tuple-element.1072), channel_id=1, source_target_pairs={{0,8},{8,0},{16,24},{24,16},{1,9},{9,1},{17,25},{25,17},{2,10},{10... | collective-permute-start | bytes 491528 | tf_op jit(solution)/shard_map/while/body/eval_jaxpr/ppermute | solution.py:22
  62.5 5.4 %collective-permute-start.2 = (bf16[640,1,128]{0,2,1:T(8,128)(2,1)S(1)}, bf16[640,1,128]{0,2,1:T(8,128)(2,1)S(1)}, u32[]{:S(2)}, u32[]{:S(2)}) collective-permute-start(bf16[640,1,128]{0,2,1:T(8,128)(2,1)S(1)} %collective-permute-done.1), channel_id=1, source_target_pairs={{0,16},{16,0},{8,24},{24,8},{1,17},{17,1},{9,25},{25,9},{2,18},{18... | collective-permute-start | bytes 491528 | tf_op jit(solution)/shard_map/while/body/eval_jaxpr/ppermute | solution.py:22
  63.7 5.9 %collective-permute-start = (bf16[640,1,128]{0,2,1:T(8,128)(2,1)}, bf16[640,1,128]{0,2,1:T(8,128)(2,1)S(1)}, u32[]{:S(2)}, u32[]{:S(2)}) collective-permute-start(bf16[640,1,128]{0,2,1:T(8,128)(2,1)} %get-tuple-element.1072), channel_id=1, source_target_pairs={{0,8},{8,16},{16,24},{1,9},{9,17},{17,25},{2,10},{10,18},{18,26},{... | collective-permute-start | bytes 491528 | tf_op jit(solution)/shard_map/while/body/eval_jaxpr/ppermute | solution.py:12
  69.6 10.4 %copy-start.1 = (bf16[1280,640]{1,0:T(8,128)(2,1)S(1)}, bf16[1280,640]{1,0:T(8,128)(2,1)}, u32[]{:S(2)}) copy-start(bf16[1280,640]{1,0:T(8,128)(2,1)} %get-tuple-element.1148) | copy-start | bytes 4915204 | tf_op jit(solution)/shard_map/while
  81.1 1.7 %collective-permute-start.1 = (bf16[640,1,128]{0,2,1:T(8,128)(2,1)}, bf16[640,1,128]{0,2,1:T(8,128)(2,1)S(1)}, u32[]{:S(2)}, u32[]{:S(2)}) collective-permute-start(bf16[640,1,128]{0,2,1:T(8,128)(2,1)} %get-tuple-element.1072), channel_id=1, source_target_pairs={{0,8},{8,0},{16,24},{24,16},{1,9},{9,1},{17,25},{25,17},{2,10},{10... | collective-permute-start | bytes 491528 | tf_op jit(solution)/shard_map/while/body/eval_jaxpr/ppermute | solution.py:22
  82.9 5.4 %collective-permute-start.2 = (bf16[640,1,128]{0,2,1:T(8,128)(2,1)S(1)}, bf16[640,1,128]{0,2,1:T(8,128)(2,1)S(1)}, u32[]{:S(2)}, u32[]{:S(2)}) collective-permute-start(bf16[640,1,128]{0,2,1:T(8,128)(2,1)S(1)} %collective-permute-done.1), channel_id=1, source_target_pairs={{0,16},{16,0},{8,24},{24,8},{1,17},{17,1},{9,25},{25,9},{2,18},{18... | collective-permute-start | bytes 491528 | tf_op jit(solution)/shard_map/while/body/eval_jaxpr/ppermute | solution.py:22
  84.1 5.9 %collective-permute-start = (bf16[640,1,128]{0,2,1:T(8,128)(2,1)}, bf16[640,1,128]{0,2,1:T(8,128)(2,1)S(1)}, u32[]{:S(2)}, u32[]{:S(2)}) collective-permute-start(bf16[640,1,128]{0,2,1:T(8,128)(2,1)} %get-tuple-element.1072), channel_id=1, source_target_pairs={{0,8},{8,16},{16,24},{1,9},{9,17},{17,25},{2,10},{10,18},{18,26},{... | collective-permute-start | bytes 491528 | tf_op jit(solution)/shard_map/while/body/eval_jaxpr/ppermute | solution.py:12
  90.0 10.4 %copy-start.1 = (bf16[1280,640]{1,0:T(8,128)(2,1)S(1)}, bf16[1280,640]{1,0:T(8,128)(2,1)}, u32[]{:S(2)}) copy-start(bf16[1280,640]{1,0:T(8,128)(2,1)} %get-tuple-element.1148) | copy-start | bytes 4915204 | tf_op jit(solution)/shard_map/while
  101.5 1.7 %collective-permute-start.1 = (bf16[640,1,128]{0,2,1:T(8,128)(2,1)}, bf16[640,1,128]{0,2,1:T(8,128)(2,1)S(1)}, u32[]{:S(2)}, u32[]{:S(2)}) collective-permute-start(bf16[640,1,128]{0,2,1:T(8,128)(2,1)} %get-tuple-element.1072), channel_id=1, source_target_pairs={{0,8},{8,0},{16,24},{24,16},{1,9},{9,1},{17,25},{25,17},{2,10},{10... | collective-permute-start | bytes 491528 | tf_op jit(solution)/shard_map/while/body/eval_jaxpr/ppermute | solution.py:22
  103.2 5.4 %collective-permute-start.2 = (bf16[640,1,128]{0,2,1:T(8,128)(2,1)S(1)}, bf16[640,1,128]{0,2,1:T(8,128)(2,1)S(1)}, u32[]{:S(2)}, u32[]{:S(2)}) collective-permute-start(bf16[640,1,128]{0,2,1:T(8,128)(2,1)S(1)} %collective-permute-done.1), channel_id=1, source_target_pairs={{0,16},{16,0},{8,24},{24,8},{1,17},{17,1},{9,25},{25,9},{2,18},{18... | collective-permute-start | bytes 491528 | tf_op jit(solution)/shard_map/while/body/eval_jaxpr/ppermute | solution.py:22
  104.4 5.9 %collective-permute-start = (bf16[640,1,128]{0,2,1:T(8,128)(2,1)}, bf16[640,1,128]{0,2,1:T(8,128)(2,1)S(1)}, u32[]{:S(2)}, u32[]{:S(2)}) collective-permute-start(bf16[640,1,128]{0,2,1:T(8,128)(2,1)} %get-tuple-element.1072), channel_id=1, source_target_pairs={{0,8},{8,16},{16,24},{1,9},{9,17},{17,25},{2,10},{10,18},{18,26},{... | collective-permute-start | bytes 491528 | tf_op jit(solution)/shard_map/while/body/eval_jaxpr/ppermute | solution.py:12
  110.3 10.4 %copy-start.2 = (bf16[1280,640]{1,0:T(8,128)(2,1)S(1)}, bf16[1280,640]{1,0:T(8,128)(2,1)}, u32[]{:S(2)}) copy-start(bf16[1280,640]{1,0:T(8,128)(2,1)} %get-tuple-element.1207) | copy-start | bytes 4915204 | tf_op jit(solution)/shard_map/while
  121.8 6.0 %collective-permute-start.3 = (bf16[640,1,128]{0,2,1:T(8,128)(2,1)}, bf16[640,1,128]{0,2,1:T(8,128)(2,1)S(1)}, u32[]{:S(2)}, u32[]{:S(2)}) collective-permute-start(bf16[640,1,128]{0,2,1:T(8,128)(2,1)} %get-tuple-element.1093), channel_id=1, source_target_pairs={{0,8},{8,16},{16,24},{1,9},{9,17},{17,25},{2,10},{10,18},{18,26},{... | collective-permute-start | bytes 491528 | tf_op jit(solution)/shard_map/while/body/eval_jaxpr/ppermute | solution.py:12
  127.9 8.5 %copy-start.2 = (bf16[1280,640]{1,0:T(8,128)(2,1)S(1)}, bf16[1280,640]{1,0:T(8,128)(2,1)}, u32[]{:S(2)}) copy-start(bf16[1280,640]{1,0:T(8,128)(2,1)} %get-tuple-element.1207) | copy-start | bytes 4915204 | tf_op jit(solution)/shard_map/while
  137.5 8.0 %collective-permute-start.3 = (bf16[640,1,128]{0,2,1:T(8,128)(2,1)}, bf16[640,1,128]{0,2,1:T(8,128)(2,1)S(1)}, u32[]{:S(2)}, u32[]{:S(2)}) collective-permute-start(bf16[640,1,128]{0,2,1:T(8,128)(2,1)} %get-tuple-element.1093), channel_id=1, source_target_pairs={{0,8},{8,16},{16,24},{1,9},{9,17},{17,25},{2,10},{10,18},{18,26},{... | collective-permute-start | bytes 491528 | tf_op jit(solution)/shard_map/while/body/eval_jaxpr/ppermute | solution.py:12
Sparse Core Ops, SparseCore 0:
  8.9 40.1 all-gather.2
where the time goes:
time: 154 us; the launch traced here: 153 us
  waiting for transfers between devices  58.7 us (38%)
  blocking collectives  30.9 us (20%)
  starting transfers between devices  23.2 us (15%)
  between operations  14.1 us (9%)
  loops' own time  10 us (6%)
  matrix products  5.6 us (4%)
  other arithmetic  5.39 us (4%)
  local copies, waits for them, and re-layouts  5.24 us (3%)
    all_gather x1, waiting for transfers between devices, per_device(): matrix_cols = lax.all_gather(weights[0], 'row', axis=0, tiled=True)  40 us
    all_gather x5, blocking collectives, advance(): lax.all_gather(activate(current, tap_mine, embed_mine, dilation, frame_co...  30.9 us
    ppermute x5, starting transfers between devices, shifted(): lax.ppermute(value, axis, [(source, source + steps) for source in range(f...  17 us
    ppermute x5, waiting for transfers between devices, shifted(): lax.ppermute(value, axis, [(source, source + steps) for source in range(f...  9.91 us
    ppermute x6, waiting for transfers between devices, from_partner(): return lax.ppermute(block, axis, route)  8.13 us
    ppermute x6, starting transfers between devices, from_partner(): return lax.ppermute(block, axis, route)  6.22 us
    another operation x1, loops' own time, per_device(): lax.fori_loop(0, first_end, lambda tick_id, carried: advance(tick_id, car...  6.05 us
    dot_general x5, matrix products, advance(): lax.dot_general(matrix_cols, activated.reshape(activated.shape[0], -1), (...  5.6 us
  transfers between devices with their start and end apart: 12, of which 12 were waited for; matrix products, arithmetic and copies ran while one was open for 1% of the time, Pallas kernels for 0%

commit v1 on v0

v1 whole, which is shorter than its diff:
```python
import functools

import jax
import jax.numpy as jnp
from jax import lax
from jax.experimental import pallas as pl
from jax.experimental.pallas import tpu as pltpu
from jax.sharding import PartitionSpec as P

MESH = pl.DeviceIdType.MESH
BLOCK = 256


def kernel(
    counts,
    times_ref,
    dilation_ref,
    latent_ref,
    weight_ref,
    taps_ref,
    table_ref,
    out_ref,
    matrix,
    states,
    active,
    params,
    results,
    skips,
    table,
    local_sem,
    left_send,
    left_recv,
    right_send,
    right_recv,
    latent_send,
    state_send,
    state_recv,
    skip_send,
    skip_recv,
):
    sections, rows, cols = counts
    section = lax.axis_index("section")
    row = lax.axis_index("row")
    col = lax.axis_index("col")
    micro, width, frames = latent_ref.shape
    depth = weight_ref.shape[0]
    steps = table_ref.shape[0]
    middle = sections // 2
    mirror = sections - 1 - section
    blocks = [(low, min(low + BLOCK, width)) for low in range(0, width, BLOCK)]
    f32 = jnp.float32

    def place(index):
        return pl.ds(pl.multiple_of(index * depth, depth), depth)

    own = pltpu.make_async_copy(weight_ref, matrix.at[place(row)], local_sem.at[0])
    own.start()
    fetch = pltpu.make_async_copy(table_ref, table, local_sem.at[1])
    fetch.start()

    has_left, has_right = row > 0, row < rows - 1
    has_next, has_last = section < sections - 1, section > 0
    is_first = section == 0
    gives_skip, takes_skip = section < middle - 1, section > middle
    barrier = pltpu.get_barrier_semaphore()

    def greet(**where):
        pl.semaphore_signal(barrier, inc=1, device_id=where, device_id_type=MESH)

    @pl.when(has_left)
    def _():
        greet(row=row - 1)

    @pl.when(has_right)
    def _():
        greet(row=row + 1)

    @pl.when(has_next)
    def _():
        for other in range(cols):
            greet(section=section + 1, col=jnp.int32(other))

    @pl.when(has_last)
    def _():
        for other in range(cols):
            greet(section=section - 1, col=jnp.int32(other))

    @pl.when(is_first)
    def _():
        for hop in range(1, cols):
            greet(col=lax.rem(col + hop, cols))

    @pl.when(jnp.logical_or(gives_skip, takes_skip))
    def _():
        greet(section=mirror)

    def flag(condition):
        return condition.astype(jnp.int32)

    expected = (
        flag(has_left)
        + flag(has_right)
        + cols * (flag(has_next) + flag(has_last))
        + (cols - 1) * flag(is_first)
        + flag(jnp.logical_or(gives_skip, takes_skip))
    )
    pl.semaphore_wait(barrier, expected)

    def move_right(hop):
        source = weight_ref if hop == 0 else matrix.at[place(row - hop)]
        return pltpu.make_async_remote_copy(
            src_ref=source,
            dst_ref=matrix.at[place(row - hop)],
            send_sem=right_send.at[hop],
            recv_sem=right_recv.at[hop],
            device_id={"row": row + 1},
            device_id_type=MESH,
        )

    def move_left(hop):
        source = weight_ref if hop == 0 else matrix.at[place(row + hop)]
        return pltpu.make_async_remote_copy(
            src_ref=source,
            dst_ref=matrix.at[place(row + hop)],
            send_sem=left_send.at[hop],
            recv_sem=left_recv.at[hop],
            device_id={"row": row - 1},
            device_id_type=MESH,
        )

    def arrived(buffer, semaphore):
        pltpu.make_async_remote_copy(
            src_ref=buffer,
            dst_ref=buffer,
            send_sem=local_sem.at[0],
            recv_sem=semaphore,
            device_id={"row": row},
            device_id_type=MESH,
        ).wait_recv()

    @pl.when(has_right)
    def _():
        move_right(0).start()

    @pl.when(has_left)
    def _():
        move_left(0).start()

    def latent_copy(m, n, hop):
        low, high = blocks[n]
        block = states.at[m, col, :, pl.ds(low, high - low)]
        return pltpu.make_async_remote_copy(
            src_ref=block,
            dst_ref=block,
            send_sem=latent_send.at[m, n, hop],
            recv_sem=state_recv.at[m, n, col],
            device_id={"col": lax.rem(col + hop, cols)},
            device_id_type=MESH,
        )

    def state_copy(m, n, hop):
        low, high = blocks[n]
        return pltpu.make_async_remote_copy(
            src_ref=results.at[m, :, pl.ds(low, high - low)],
            dst_ref=states.at[m, col, :, pl.ds(low, high - low)],
            send_sem=state_send.at[m, n, hop],
            recv_sem=state_recv.at[m, n, col],
            device_id={"section": section + 1, "col": lax.rem(col + hop, cols)},
            device_id_type=MESH,
        )

    def skip_copy(m, n):
        low, high = blocks[n]
        return pltpu.make_async_remote_copy(
            src_ref=results.at[m, :, pl.ds(low, high - low)],
            dst_ref=skips.at[m, :, pl.ds(low, high - low)],
            send_sem=skip_send.at[m, n],
            recv_sem=skip_recv.at[m, n],
            device_id={"section": mirror},
            device_id_type=MESH,
        )

    @pl.when(is_first)
    def _():
        for m in range(micro):
            states[m, col] = latent_ref[m].astype(f32).T.astype(jnp.bfloat16)
            for hop in range(1, cols):
                for n in range(len(blocks)):
                    latent_copy(m, n, hop).start()

    @pl.when(section < middle)
    def _():
        skips[...] = jnp.zeros_like(skips)

    dilation = dilation_ref[0]
    target = lax.broadcasted_iota(jnp.int32, (frames, frames), 0)
    origin = lax.broadcasted_iota(jnp.int32, (frames, frames), 1)
    earlier = jnp.where(origin == target - dilation, 1.0, 0.0).astype(jnp.bfloat16)
    later = jnp.where(origin == target + dilation, 1.0, 0.0).astype(jnp.bfloat16)

    slot = lax.broadcasted_iota(jnp.int32, (16, steps), 0)
    number = lax.broadcasted_iota(jnp.int32, (16, steps), 1)
    chosen = jnp.zeros((16, steps), f32)
    for m in range(micro):
        hit = jnp.logical_and(slot == m, number == times_ref[m])
        chosen = jnp.where(hit, 1.0, chosen)
    fetch.wait()
    embedding = jnp.dot(chosen.astype(jnp.bfloat16), table[...], preferred_element_type=f32)
    for other in range(cols):
        span = slice(other * width, (other + 1) * width)
        params[other, 0:3, :] = taps_ref[:, span]
        params[other, 3 : 3 + micro, :] = embedding[0:micro, span]

    def activate(m, is_latent):
        for hop in range(cols):
            other = lax.rem(col + hop, cols)
            for n, (low, high) in enumerate(blocks):
                if not (is_latent and hop == 0):
                    arrived(
                        states.at[m, other, :, pl.ds(low, high - low)],
                        state_recv.at[m, n, other],
                    )
                value = states[m, other, :, low:high]
                summed = (
                    params[other, 0:1, low:high]
                    * jnp.dot(earlier, value, preferred_element_type=f32)
                    + params[other, 1:2, low:high] * value.astype(f32)
                    + params[other, 2:3, low:high]
                    * jnp.dot(later, value, preferred_element_type=f32)
                    + params[other, 3 + m : 4 + m, low:high]
                )
                active[m, other, :, low:high] = (summed / (1.0 + jnp.exp(-summed))).astype(
                    jnp.bfloat16
                )

    @pl.when(is_first)
    def _():
        for m in range(micro):
            activate(m, True)

    own.wait()
    for hop in range(1, rows):

        @pl.when(row - hop >= 0)
        def _():
            arrived(matrix.at[place(row - hop)], right_recv.at[hop - 1])

            @pl.when(has_right)
            def _():
                move_right(hop).start()

        @pl.when(row + hop < rows)
        def _():
            arrived(matrix.at[place(row + hop)], left_recv.at[hop - 1])

            @pl.when(has_left)
            def _():
                move_left(hop).start()

    for m in range(micro):

        @pl.when(has_last)
        def _():
            activate(m, False)

        @pl.when(section == middle)
        def _():
            skips[m] = states[m, col]

        for n, (low, high) in enumerate(blocks):
            mixed = jnp.dot(
                active[m, 0], matrix[0:width, low:high], preferred_element_type=f32
            )
            for other in range(1, cols):
                mixed += jnp.dot(
                    active[m, other],
                    matrix[other * width : (other + 1) * width, low:high],
                    preferred_element_type=f32,
                )

            @pl.when(takes_skip)
            def _():
                arrived(skips.at[m, :, pl.ds(low, high - low)], skip_recv.at[m, n])

            results[m, :, low:high] = (
                states[m, col, :, low:high].astype(f32)
                + mixed
                + skips[m, :, low:high].astype(f32)
            ).astype(jnp.bfloat16)

            @pl.when(has_next)
            def _():
                for hop in reversed(range(cols)):
                    state_copy(m, n, hop).start()

            @pl.when(gives_skip)
            def _():
                skip_copy(m, n).start()

        out_ref[m] = results[m].astype(f32).T.astype(jnp.bfloat16)

    @pl.when(is_first)
    def _():
        for m in range(micro):
            for hop in range(1, cols):
                for n in range(len(blocks)):
                    latent_copy(m, n, hop).wait_send()

    @pl.when(has_next)
    def _():
        for m in range(micro):
            for hop in range(cols):
                for n in range(len(blocks)):
                    state_copy(m, n, hop).wait_send()

    @pl.when(gives_skip)
    def _():
        for m in range(micro):
            for n in range(len(blocks)):
                skip_copy(m, n).wait_send()

    for hop in range(rows - 1):

        @pl.when(jnp.logical_and(has_right, row - hop >= 0))
        def _():
            move_right(hop).wait_send()

        @pl.when(jnp.logical_and(has_left, row + hop < rows))
        def _():
            move_left(hop).wait_send()


def per_device(counts, latents, timesteps, weights, taps, time_table, dilations):
    sections, rows, cols = counts
    micro, width, _, frames = latents.shape
    depth = weights.shape[1]
    steps, channels = time_table.shape[1:]
    count = pl.cdiv(width, BLOCK)
    bf16 = jnp.bfloat16
    dma = pltpu.SemaphoreType.DMA
    vmem = pl.BlockSpec(memory_space=pltpu.VMEM)
    smem = pl.BlockSpec(memory_space=pltpu.SMEM)
    hbm = pl.BlockSpec(memory_space=pl.ANY)
    out = pl.pallas_call(
        functools.partial(kernel, counts),
        out_shape=jax.ShapeDtypeStruct((micro, width, frames), bf16),
        in_specs=[smem, smem, vmem, hbm, vmem, hbm],
        out_specs=vmem,
        scratch_shapes=[
            pltpu.VMEM((channels, width), bf16),
            pltpu.VMEM((micro, cols, frames, width), bf16),
            pltpu.VMEM((micro, cols, frames, width), bf16),
            pltpu.VMEM((cols, 8, width), jnp.float32),
            pltpu.VMEM((micro, frames, width), bf16),
            pltpu.VMEM((micro, frames, width), bf16),
            pltpu.VMEM((steps, channels), bf16),
            dma((2,)),
            dma((rows,)),
            dma((rows,)),
            dma((rows,)),
            dma((rows,)),
            dma((micro, count, cols)),
            dma((micro, count, cols)),
            dma((micro, count, cols)),
            dma((micro, count)),
            dma((micro, count)),
        ],
        compiler_params=pltpu.CompilerParams(
            collective_id=0, has_side_effects=True, vmem_limit_bytes=32 * 2**20
        ),
    )(
        timesteps,
        dilations,
        latents.reshape(micro, width, frames),
        weights[0],
        taps[0],
        time_table[0],
    )
    return out.reshape(1, micro, width, 1, frames)


def solution(mesh):
    counts = tuple(mesh.shape[axis] for axis in ("section", "row", "col"))
    in_specs = (
        P(None, "col", "row", None),
        P(),
        P("section", "row", "col"),
        P("section", None, None),
        P("section", None, None),
        P("section"),
    )
    return jax.shard_map(
        functools.partial(per_device, counts),
        mesh=mesh,
        in_specs=in_specs,
        out_specs=P("section", None, "col", "row", None),
        check_vma=False,
    )
```

time: 154 us -> 64.1 us (0.42)
  the two profiles are of different devices: /device:TPU:1 before, /device:TPU:3 now
where the time goes in v1:
time: 64.1 us; the launch traced here: 63.8 us
  Pallas kernels  57.3 us (89%)
  local copies, waits for them, and re-layouts  5.8 us (9%)
  between operations  0.67 us (1%)
    pallas_call x1, Pallas kernels, per_device(): pl.pallas_call(functools.partial(kernel, counts), out_shape=jax.ShapeDtyp...  57.3 us
    unnamed x10, local copies, waits for them, and re-layouts  5.8 us

profile of v1, /device:TPU:3, one launch (start us, length us, event | category | flops | bytes accessed | tf_op | source)
XLA Modules:
  0.0 63.8 jit_solution(3235324334873393791)
XLA Ops:
  0.7 0.7 %copy.10 = f32[1,3,1280]{2,1,0:T(4,128)S(1)} copy(f32[1,3,1280]{2,0,1:T(1,128)} %param.9) | data formatting | bytes 30720
  1.4 0.0 copy-start
  1.4 1.7 %copy-done = bf16[1,1000,1280]{2,1,0:T(8,128)(2,1)S(1)} copy-done((bf16[1,1000,1280]{2,1,0:T(8,128)(2,1)S(1)}, bf16[1,1000,1280]{2,1,0:T(8,128)(2,1)}, u32[]{:S(2)}) %copy-start) | copy-done | bytes 2560024
  3.1 0.0 copy-start.1
  3.1 1.0 %copy-done.1 = bf16[1,320,640]{2,1,0:T(8,128)(2,1)S(1)} copy-done((bf16[1,320,640]{2,1,0:T(8,128)(2,1)S(1)}, bf16[1,320,640]{2,1,0:T(8,128)(2,1)}, u32[]{:S(2)}) %copy-start.1) | copy-done | bytes 409624
  4.1 0.0 copy-start.2
  4.1 1.0 %copy-done.2 = bf16[2,640,1,128]{3,1,2,0:T(8,128)(2,1)S(1)} copy-done((bf16[2,640,1,128]{3,1,2,0:T(8,128)(2,1)S(1)}, bf16[2,640,1,128]{3,1,2,0:T(8,128)(2,1)}, u32[]{:S(2)}) %copy-start.2) | copy-done | bytes 327704
  5.1 0.0 copy-start.3
  5.1 0.7 %copy-done.3 = s32[2]{0:T(128)S(1)} copy-done((s32[2]{0:T(128)S(1)}, s32[2]{0:T(128)}, u32[]{:S(2)}) %copy-start.3) | copy-done | bytes 32
  5.7 57.3 %shard_map.64 = bf16[2,640,128]{2,1,0:T(8,128)(2,1)S(1)} custom-call(s32[2]{0:T(128)S(1)} %copy-done.3, s32[1]{0:T(128)S(6)} %copy.12.dilation_ref, bf16[2,640,128]{2,1,0:T(8,128)(2,1)S(1)} %bitcast.12, bf16[320,640]{1,0:T(8,128)(2,1)S(1)} %bitcast.11, f32[3,1280]{1,0:T(4,128)S(1)} %bitcast.13, bf16[1000,1280]{1,0:T(8,128)(2,1)S(1)} %bitcast.9), custom_call_target="tpu_custom_call" | custom-call | tf_op jit(solution)/shard_map/pallas_call | solution.py:344
  63.0 0.7 %copy.13 = bf16[1,2,640,1,128]{4,2,3,1,0:T(8,128)(2,1)} copy(bf16[1,2,640,1,128]{4,2,3,1,0:T(8,128)(2,1)S(1)} %bitcast.10) | data formatting | bytes 655360
Async XLA Ops:
  1.4 1.7 %copy-start = (bf16[1,1000,1280]{2,1,0:T(8,128)(2,1)S(1)}, bf16[1,1000,1280]{2,1,0:T(8,128)(2,1)}, u32[]{:S(2)}) copy-start(bf16[1,1000,1280]{2,1,0:T(8,128)(2,1)} %param.10) | copy-start | bytes 7680004
  3.1 1.0 %copy-start.1 = (bf16[1,320,640]{2,1,0:T(8,128)(2,1)S(1)}, bf16[1,320,640]{2,1,0:T(8,128)(2,1)}, u32[]{:S(2)}) copy-start(bf16[1,320,640]{2,1,0:T(8,128)(2,1)} %param.8) | copy-start | bytes 1228804
  4.1 1.0 %copy-start.2 = (bf16[2,640,1,128]{3,1,2,0:T(8,128)(2,1)S(1)}, bf16[2,640,1,128]{3,1,2,0:T(8,128)(2,1)}, u32[]{:S(2)}) copy-start(bf16[2,640,1,128]{3,1,2,0:T(8,128)(2,1)} %param.6) | copy-start | bytes 983044
  5.1 0.7 %copy-start.3 = (s32[2]{0:T(128)S(1)}, s32[2]{0:T(128)}, u32[]{:S(2)}) copy-start(s32[2]{0:T(128)} %times_ref.1) | copy-start | bytes 28

commit v2 on v1

--- a/solution.py
+++ b/solution.py
@@ -9,16 +9,17 @@
 
 MESH = pl.DeviceIdType.MESH
 BLOCK = 256
+PIECES = 2
 
 
 def kernel(
     counts,
     times_ref,
     dilation_ref,
-    latent_ref,
-    weight_ref,
-    taps_ref,
-    table_ref,
+    latent_hbm,
+    weight_hbm,
+    taps_hbm,
+    table_hbm,
     out_ref,
     matrix,
     states,
@@ -27,6 +28,8 @@
     results,
     skips,
     table,
+    latent_ref,
+    taps_ref,
     local_sem,
     left_send,
     left_recv,
@@ -43,20 +46,27 @@
     row = lax.axis_index("row")
     col = lax.axis_index("col")
     micro, width, frames = latent_ref.shape
+    weight_ref = weight_hbm.at[0]
     depth = weight_ref.shape[0]
-    steps = table_ref.shape[0]
+    steps = table.shape[0]
     middle = sections // 2
     mirror = sections - 1 - section
     blocks = [(low, min(low + BLOCK, width)) for low in range(0, width, BLOCK)]
     f32 = jnp.float32
 
-    def place(index):
-        return pl.ds(pl.multiple_of(index * depth, depth), depth)
-
-    own = pltpu.make_async_copy(weight_ref, matrix.at[place(row)], local_sem.at[0])
+    piece = depth // PIECES
+
+    def place(index, q):
+        return pl.ds(pl.multiple_of(index * depth + q * piece, piece), piece)
+
+    own = pltpu.make_async_copy(weight_ref, matrix.at[pl.ds(pl.multiple_of(row * depth, depth), depth)], local_sem.at[0])
     own.start()
-    fetch = pltpu.make_async_copy(table_ref, table, local_sem.at[1])
+    fetch = pltpu.make_async_copy(table_hbm.at[0], table, local_sem.at[1])
     fetch.start()
+    fetch_latents = pltpu.make_async_copy(latent_hbm, latent_ref, local_sem.at[2])
+    fetch_latents.start()
+    fetch_taps = pltpu.make_async_copy(taps_hbm, taps_ref, local_sem.at[3])
+    fetch_taps.start()
 
     has_left, has_right = row > 0, row < rows - 1
     has_next, has_last = section < sections - 1, section > 0
@@ -106,24 +116,24 @@
     )
     pl.semaphore_wait(barrier, expected)
 
-    def move_right(hop):
-        source = weight_ref if hop == 0 else matrix.at[place(row - hop)]
+    def move_right(hop, q):
+        source = weight_ref.at[pl.ds(q * piece, piece)] if hop == 0 else matrix.at[place(row - hop, q)]
         return pltpu.make_async_remote_copy(
             src_ref=source,
-            dst_ref=matrix.at[place(row - hop)],
-            send_sem=right_send.at[hop],
-            recv_sem=right_recv.at[hop],
+            dst_ref=matrix.at[place(row - hop, q)],
+            send_sem=right_send.at[hop, q],
+            recv_sem=right_recv.at[hop, q],
             device_id={"row": row + 1},
             device_id_type=MESH,
         )
 
-    def move_left(hop):
-        source = weight_ref if hop == 0 else matrix.at[place(row + hop)]
+    def move_left(hop, q):
+        source = weight_ref.at[pl.ds(q * piece, piece)] if hop == 0 else matrix.at[place(row + hop, q)]
         return pltpu.make_async_remote_copy(
             src_ref=source,
-            dst_ref=matrix.at[place(row + hop)],
-            send_sem=left_send.at[hop],
-            recv_sem=left_recv.at[hop],
+            dst_ref=matrix.at[place(row + hop, q)],
+            send_sem=left_send.at[hop, q],
+            recv_sem=left_recv.at[hop, q],
             device_id={"row": row - 1},
             device_id_type=MESH,
         )
@@ -140,11 +150,13 @@
 
     @pl.when(has_right)
     def _():
-        move_right(0).start()
+        for q in range(PIECES):
+            move_right(0, q).start()
 
     @pl.when(has_left)
     def _():
-        move_left(0).start()
+        for q in range(PIECES):
+            move_left(0, q).start()
 
     def latent_copy(m, n, hop):
         low, high = blocks[n]
@@ -180,6 +192,8 @@
             device_id_type=MESH,
         )
 
+    fetch_latents.wait()
+
     @pl.when(is_first)
     def _():
         for m in range(micro):
@@ -192,11 +206,33 @@
     def _():
         skips[...] = jnp.zeros_like(skips)
 
+    def forward(hop):
+        for q in range(PIECES):
+
+            @pl.when(row - hop >= 0)
+            def _():
+                arrived(matrix.at[place(row - hop, q)], right_recv.at[hop - 1, q])
+
+                @pl.when(has_right)
+                def _():
+                    move_right(hop, q).start()
+
+            @pl.when(row + hop < rows)
+            def _():
+                arrived(matrix.at[place(row + hop, q)], left_recv.at[hop - 1, q])
+
+                @pl.when(has_left)
+                def _():
+                    move_left(hop, q).start()
+
+    if rows > 1:
+        forward(1)
+
     dilation = dilation_ref[0]
-    target = lax.broadcasted_iota(jnp.int32, (frames, frames), 0)
-    origin = lax.broadcasted_iota(jnp.int32, (frames, frames), 1)
-    earlier = jnp.where(origin == target - dilation, 1.0, 0.0).astype(jnp.bfloat16)
-    later = jnp.where(origin == target + dilation, 1.0, 0.0).astype(jnp.bfloat16)
+    line = lax.broadcasted_iota(jnp.int32, (2 * frames, frames), 0)
+    origin = lax.broadcasted_iota(jnp.int32, (2 * frames, frames), 1)
+    wanted = jnp.where(line < frames, line - dilation, line - frames + dilation)
+    shift = jnp.where(origin == wanted, 1.0, 0.0).astype(jnp.bfloat16)
 
     slot = lax.broadcasted_iota(jnp.int32, (16, steps), 0)
     number = lax.broadcasted_iota(jnp.int32, (16, steps), 1)
@@ -205,11 +241,13 @@
         hit = jnp.logical_and(slot == m, number == times_ref[m])
         chosen = jnp.where(hit, 1.0, chosen)
     fetch.wait()
+    fetch_taps.wait()
     embedding = jnp.dot(chosen.astype(jnp.bfloat16), table[...], preferred_element_type=f32)
     for other in range(cols):
         span = slice(other * width, (other + 1) * width)
-        params[other, 0:3, :] = taps_ref[:, span]
-        params[other, 3 : 3 + micro, :] = embedding[0:micro, span]
+        for tap in range(3):
+            params[other, tap : tap + 1, :] = 0.5 * taps_ref[tap, :, span]
+        params[other, 3 : 3 + micro, :] = 0.5 * embedding[0:micro, span]
 
     def activate(m, is_latent):
         for hop in range(cols):
@@ -221,42 +259,28 @@
                         state_recv.at[m, n, other],
                     )
                 value = states[m, other, :, low:high]
-                summed = (
-                    params[other, 0:1, low:high]
-                    * jnp.dot(earlier, value, preferred_element_type=f32)
+                moved = jnp.dot(shift, value, preferred_element_type=f32)
+                half = (
+                    params[other, 0:1, low:high] * moved[:frames]
                     + params[other, 1:2, low:high] * value.astype(f32)
-                    + params[other, 2:3, low:high]
-                    * jnp.dot(later, value, preferred_element_type=f32)
+                    + params[other, 2:3, low:high] * moved[frames:]
                     + params[other, 3 + m : 4 + m, low:high]
                 )
-                active[m, other, :, low:high] = (summed / (1.0 + jnp.exp(-summed))).astype(
+                active[m, other, :, low:high] = (half + half * jnp.tanh(half)).astype(
                     jnp.bfloat16
                 )
 
-    @pl.when(is_first)
-    def _():
-        for m in range(micro):
-            activate(m, True)
+    for turn in range(max(micro, rows - 2)):
+        if turn < micro:
+
+            @pl.when(is_first)
+            def _():
+                activate(turn, True)
+
+        if turn < rows - 2:
+            forward(turn + 2)
 
     own.wait()
-    for hop in range(1, rows):
-
-        @pl.when(row - hop >= 0)
-        def _():
-            arrived(matrix.at[place(row - hop)], right_recv.at[hop - 1])
-
-            @pl.when(has_right)
-            def _():
-                move_right(hop).start()
-
-        @pl.when(row + hop < rows)
-        def _():
-            arrived(matrix.at[place(row + hop)], left_recv.at[hop - 1])
-
-            @pl.when(has_left)
-            def _():
-                move_left(hop).start()
-
     for m in range(micro):
 
         @pl.when(has_last)
@@ -323,11 +347,13 @@
 
         @pl.when(jnp.logical_and(has_right, row - hop >= 0))
         def _():
-            move_right(hop).wait_send()
+            for q in range(PIECES):
+                move_right(hop, q).wait_send()
 
         @pl.when(jnp.logical_and(has_left, row + hop < rows))
         def _():
-            move_left(hop).wait_send()
+            for q in range(PIECES):
+                move_left(hop, q).wait_send()
 
 
 def per_device(counts, latents, timesteps, weights, taps, time_table, dilations):
@@ -344,7 +370,7 @@
     out = pl.pallas_call(
         functools.partial(kernel, counts),
         out_shape=jax.ShapeDtypeStruct((micro, width, frames), bf16),
-        in_specs=[smem, smem, vmem, hbm, vmem, hbm],
+        in_specs=[smem, smem, hbm, hbm, hbm, hbm],
         out_specs=vmem,
         scratch_shapes=[
             pltpu.VMEM((channels, width), bf16),
@@ -354,11 +380,13 @@
             pltpu.VMEM((micro, frames, width), bf16),
             pltpu.VMEM((micro, frames, width), bf16),
             pltpu.VMEM((steps, channels), bf16),
-            dma((2,)),
-            dma((rows,)),
-            dma((rows,)),
-            dma((rows,)),
-            dma((rows,)),
+            pltpu.VMEM((micro, width, frames), bf16),
+            pltpu.VMEM((3, 1, channels), jnp.float32),
+            dma((4,)),
+            dma((rows, PIECES)),
+            dma((rows, PIECES)),
+            dma((rows, PIECES)),
+            dma((rows, PIECES)),
             dma((micro, count, cols)),
             dma((micro, count, cols)),
             dma((micro, count, cols)),
@@ -366,15 +394,15 @@
             dma((micro, count)),
         ],
         compiler_params=pltpu.CompilerParams(
-            collective_id=0, has_side_effects=True, vmem_limit_bytes=32 * 2**20
+            collective_id=0, has_side_effects=True, vmem_limit_bytes=60 * 2**20
         ),
     )(
         timesteps,
         dilations,
         latents.reshape(micro, width, frames),
-        weights[0],
-        taps[0],
-        time_table[0],
+        weights,
+        taps.reshape(3, 1, channels),
+        time_table,
     )
     return out.reshape(1, micro, width, 1, frames)
 

time: 64.1 us -> 55.9 us (0.87)
  local copies, waits for them, and re-layouts: 5.8 us -> 1.72 us
  Pallas kernels: 57.3 us -> 53.3 us
    unnamed x10 -> x1, local copies, waits for them, and re-layouts: 5.8 us -> 1.72 us
    pallas_call x1, Pallas kernels: 57.3 us -> 53.3 us  [per_device(): pl.pallas_call(functools.partial(kernel, counts), out_shape=jax.ShapeDtyp...]
where the time goes in v2:
time: 55.9 us; the launch traced here: 55.7 us
  Pallas kernels  53.3 us (95%)
  local copies, waits for them, and re-layouts  1.72 us (3%)
  between operations  0.66 us (1%)
    pallas_call x1, Pallas kernels, per_device(): pl.pallas_call(functools.partial(kernel, counts), out_shape=jax.ShapeDtyp...  53.3 us
    unnamed x1, local copies, waits for them, and re-layouts  1.72 us

profile of v2, /device:TPU:3, one launch (start us, length us, event | category | flops | bytes accessed | tf_op | source)
XLA Modules:
  0.0 55.7 jit_solution(1472062047698752272)
XLA Ops:
  0.7 53.3 %shard_map.64 = bf16[2,640,128]{2,1,0:T(8,128)(2,1)} custom-call(s32[2]{0:T(128)} %times_ref.1, s32[1]{0:T(128)S(6)} %copy.9.dilation_ref, bf16[2,640,128]{2,1,0:T(8,128)(2,1)} %bitcast.6, bf16[1,320,640]{2,1,0:T(8,128)(2,1)} %weight_hbm.1, f32[3,1,1280]{2,1,0:T(1,128)} %bitcast.7, bf16[1,1000,1280]{2,1,0:T(8,128)(2,1)} %table_hbm.1), custom_call_target="tpu_custom_call" | custom-call | tf_op jit(solution)/shard_map/pallas_call | solution.py:370
  54.0 1.7 %copy.10 = bf16[1,2,640,1,128]{4,2,3,1,0:T(8,128)(2,1)} copy(bf16[1,2,640,1,128]{4,2,3,1,0:T(8,128)(2,1)} %bitcast.5) | data formatting | bytes 655360

commit v3 on v2

--- a/solution.py
+++ b/solution.py
@@ -31,6 +31,7 @@
     latent_ref,
     taps_ref,
     local_sem,
+    turn_sem,
     left_send,
     left_recv,
     right_send,
@@ -148,6 +149,13 @@
             device_id_type=MESH,
         ).wait_recv()
 
+    goes_first = jnp.logical_and(lax.rem(section, 2) == 0, has_next)
+    goes_second = lax.rem(section, 2) == 1
+
+    @pl.when(goes_second)
+    def _():
+        pl.semaphore_wait(turn_sem, 1)
+
     @pl.when(has_right)
     def _():
         for q in range(PIECES):
@@ -227,6 +235,22 @@
 
     if rows > 1:
         forward(1)
+
+        @pl.when(has_right)
+        def _():
+            for q in range(PIECES):
+                move_right(0, q).wait_send()
+
+        @pl.when(has_left)
+        def _():
+            for q in range(PIECES):
+                move_left(0, q).wait_send()
+
+    @pl.when(goes_first)
+    def _():
+        pl.semaphore_signal(
+            turn_sem, inc=1, device_id={"section": section + 1}, device_id_type=MESH
+        )
 
     dilation = dilation_ref[0]
     line = lax.broadcasted_iota(jnp.int32, (2 * frames, frames), 0)
@@ -250,9 +274,9 @@
         params[other, 3 : 3 + micro, :] = 0.5 * embedding[0:micro, span]
 
     def activate(m, is_latent):
-        for hop in range(cols):
-            other = lax.rem(col + hop, cols)
-            for n, (low, high) in enumerate(blocks):
+        for n, (low, high) in enumerate(blocks):
+            for hop in range(cols):
+                other = lax.rem(col + hop, cols)
                 if not (is_latent and hop == 0):
                     arrived(
                         states.at[m, other, :, pl.ds(low, high - low)],
@@ -321,6 +345,8 @@
             def _():
                 skip_copy(m, n).start()
 
+
+    for m in range(micro):
         out_ref[m] = results[m].astype(f32).T.astype(jnp.bfloat16)
 
     @pl.when(is_first)
@@ -343,7 +369,7 @@
             for n in range(len(blocks)):
                 skip_copy(m, n).wait_send()
 
-    for hop in range(rows - 1):
+    for hop in range(1, rows - 1):
 
         @pl.when(jnp.logical_and(has_right, row - hop >= 0))
         def _():
@@ -383,6 +409,7 @@
             pltpu.VMEM((micro, width, frames), bf16),
             pltpu.VMEM((3, 1, channels), jnp.float32),
             dma((4,)),
+            pltpu.SemaphoreType.REGULAR,
             dma((rows, PIECES)),
             dma((rows, PIECES)),
             dma((rows, PIECES)),

time: 55.9 us -> 53.7 us (0.961)
  Pallas kernels: 53.3 us -> 51.1 us
    pallas_call x1, Pallas kernels: 53.3 us -> 51.1 us  [per_device(): pl.pallas_call(functools.partial(kernel, counts), out_shape=jax.ShapeDtyp...]
where the time goes in v3:
time: 53.7 us; the launch traced here: 53.5 us
  Pallas kernels  51.1 us (95%)
  local copies, waits for them, and re-layouts  1.72 us (3%)
  between operations  0.66 us (1%)
    pallas_call x1, Pallas kernels, per_device(): pl.pallas_call(functools.partial(kernel, counts), out_shape=jax.ShapeDtyp...  51.1 us
    unnamed x1, local copies, waits for them, and re-layouts  1.72 us

profile of v3, /device:TPU:3, one launch (start us, length us, event | category | flops | bytes accessed | tf_op | source)
XLA Modules:
  0.0 53.5 jit_solution(906360493285274943)
XLA Ops:
  0.7 51.1 %shard_map.64 = bf16[2,640,128]{2,1,0:T(8,128)(2,1)} custom-call(s32[2]{0:T(128)} %times_ref.1, s32[1]{0:T(128)S(6)} %copy.9.dilation_ref, bf16[2,640,128]{2,1,0:T(8,128)(2,1)} %bitcast.6, bf16[1,320,640]{2,1,0:T(8,128)(2,1)} %weight_hbm.1, f32[3,1,1280]{2,1,0:T(1,128)} %bitcast.7, bf16[1,1000,1280]{2,1,0:T(8,128)(2,1)} %table_hbm.1), custom_call_target="tpu_custom_call" | custom-call | tf_op jit(solution)/shard_map/pallas_call | solution.py:396
  51.8 1.7 %copy.10 = bf16[1,2,640,1,128]{4,2,3,1,0:T(8,128)(2,1)} copy(bf16[1,2,640,1,128]{4,2,3,1,0:T(8,128)(2,1)} %bitcast.5) | data formatting | bytes 655360

commit v4 on v3

--- a/solution.py
+++ b/solution.py
@@ -8,8 +8,8 @@
 from jax.sharding import PartitionSpec as P
 
 MESH = pl.DeviceIdType.MESH
-BLOCK = 256
-PIECES = 2
+BLOCK = 640
+PIECES = 5
 
 
 def kernel(

time: 53.7 us -> 52.3 us (0.974)
  Pallas kernels: 51.1 us -> 49.8 us
    pallas_call x1, Pallas kernels: 51.1 us -> 49.8 us  [per_device(): pl.pallas_call(functools.partial(kernel, counts), out_shape=jax.ShapeDtyp...]
where the time goes in v4:
time: 52.3 us; the launch traced here: 52.1 us
  Pallas kernels  49.8 us (95%)
  local copies, waits for them, and re-layouts  1.72 us (3%)
  between operations  0.66 us (1%)
    pallas_call x1, Pallas kernels, per_device(): pl.pallas_call(functools.partial(kernel, counts), out_shape=jax.ShapeDtyp...  49.8 us
    unnamed x1, local copies, waits for them, and re-layouts  1.72 us

profile of v4, /device:TPU:3, one launch (start us, length us, event | category | flops | bytes accessed | tf_op | source)
XLA Modules:
  0.0 52.1 jit_solution(5313438146974986351)
XLA Ops:
  0.7 49.8 %shard_map.64 = bf16[2,640,128]{2,1,0:T(8,128)(2,1)} custom-call(s32[2]{0:T(128)} %times_ref.1, s32[1]{0:T(128)S(6)} %copy.9.dilation_ref, bf16[2,640,128]{2,1,0:T(8,128)(2,1)} %bitcast.6, bf16[1,320,640]{2,1,0:T(8,128)(2,1)} %weight_hbm.1, f32[3,1,1280]{2,1,0:T(1,128)} %bitcast.7, bf16[1,1000,1280]{2,1,0:T(8,128)(2,1)} %table_hbm.1), custom_call_target="tpu_custom_call" | custom-call | tf_op jit(solution)/shard_map/pallas_call | solution.py:396
  50.4 1.7 %copy.10 = bf16[1,2,640,1,128]{4,2,3,1,0:T(8,128)(2,1)} copy(bf16[1,2,640,1,128]{4,2,3,1,0:T(8,128)(2,1)} %bitcast.5) | data formatting | bytes 655360

commit v5 on v4

--- a/solution.py
+++ b/solution.py
@@ -295,14 +295,14 @@
                 )
 
     for turn in range(max(micro, rows - 2)):
-        if turn < micro:
-
-            @pl.when(is_first)
-            def _():
-                activate(turn, True)
-
         if turn < rows - 2:
             forward(turn + 2)
+
+        if turn < micro:
+
+            @pl.when(is_first)
+            def _():
+                activate(turn, True)
 
     own.wait()
     for m in range(micro):
@@ -338,7 +338,7 @@
 
             @pl.when(has_next)
             def _():
-                for hop in reversed(range(cols)):
+                for hop in range(cols):
                     state_copy(m, n, hop).start()
 
             @pl.when(gives_skip)

time: 52.3 us -> 52.1 us (level)
  no operation moved by 1% of the time
where the time goes in v5:
time: 52.1 us; the launch traced here: 51.8 us
  Pallas kernels  49.4 us (95%)
  local copies, waits for them, and re-layouts  1.72 us (3%)
  between operations  0.66 us (1%)
    pallas_call x1, Pallas kernels, per_device(): pl.pallas_call(functools.partial(kernel, counts), out_shape=jax.ShapeDtyp...  49.4 us
    unnamed x1, local copies, waits for them, and re-layouts  1.72 us

profile of v5, /device:TPU:3, one launch (start us, length us, event | category | flops | bytes accessed | tf_op | source)
XLA Modules:
  0.0 51.8 jit_solution(17892410433127736936)
XLA Ops:
  0.7 49.4 %shard_map.64 = bf16[2,640,128]{2,1,0:T(8,128)(2,1)} custom-call(s32[2]{0:T(128)} %times_ref.1, s32[1]{0:T(128)S(6)} %copy.9.dilation_ref, bf16[2,640,128]{2,1,0:T(8,128)(2,1)} %bitcast.6, bf16[1,320,640]{2,1,0:T(8,128)(2,1)} %weight_hbm.1, f32[3,1,1280]{2,1,0:T(1,128)} %bitcast.7, bf16[1,1000,1280]{2,1,0:T(8,128)(2,1)} %table_hbm.1), custom_call_target="tpu_custom_call" | custom-call | tf_op jit(solution)/shard_map/pallas_call | solution.py:396
  50.1 1.7 %copy.10 = bf16[1,2,640,1,128]{4,2,3,1,0:T(8,128)(2,1)} copy(bf16[1,2,640,1,128]{4,2,3,1,0:T(8,128)(2,1)} %bitcast.5) | data formatting | bytes 655360
